TPU v7x, 32 devices: a whole 2x2x4 slice. The times are simulated.
32 devices in a mesh: users: 2 (over x), hist: 8 (over z, y), head: 2 (over core).
Axes of the slice: x: 2, y: 2, z: 4, core: 2. Of those that a mesh axis runs over, the one named last changes fastest.
Arguments:
- candidates: bfloat16 [2048, 512], P(('users', 'hist')), parts along dimension 0, may hold values from -6 to 6
- key_cache: bfloat16 [2, 32768, 512], P(None, ('users', 'hist'), 'head'), parts along dimension 1, may hold values from -6 to 6
- value_cache: bfloat16 [2, 32768, 512], P(None, ('users', 'hist'), 'head'), parts along dimension 1, may hold values from -6 to 6
- w_in: bfloat16 [2, 512, 4, 512], P(None, None, None, 'head'), may hold values from -0.25 to 0.25
- w_out: bfloat16 [2, 512, 512], P(None, 'head'), may hold values from -0.25 to 0.25
- rab_table: float32 [2, 32, 8], P(None, None, 'head'), may hold values from -4 to 4
- hist_len: int32 [16], P(('users', 'hist')), parts along dimension 0, may hold values from 1 to 2048, 8192 in all
- hist_bucket: int32 [32768], P(('users', 'hist')), parts along dimension 0, may hold values from 0 to 31
- visible: int32 [8, 128], P(None, ('users', 'hist')), parts along dimension 1, may hold values 0 or 1
Outputs:
- candidate_out: bfloat16 [2048, 512], P(('users', 'hist')), parts along dimension 0
There are 2 independent parts, one for each index of `users`. A program takes and returns all parts, laid end to end along the dimension named above; an argument that names none is the same for every part. Nothing has to cross between parts.
Inputs may be any that keep to these rules, and one draw needn't show every extreme that they name: `hist_len`: entry s counts the valid events at the start of history shard s; the entries sum to 8192 and the largest is 2048. visible[m, b] is 1 where microbatch m sees history events b * 256 to (b + 1) * 256 - 1.
All inputs are finite; a program needn't handle non-finite values.
Results may differ from a plain program's by a relative error of at most 0.019.
Values may be sent and summed in bfloat16 or wider, within the bound.
No kernel may reach another device: no remote copies, remote signals or barrier semaphores. Data moves between devices by JAX's collectives and lax.ppermute only.
A program may use at most 64 MiB of HBM per device.

v0:
```python
import jax
import jax.numpy as jnp
from jax import lax
from jax.sharding import PartitionSpec as P

D = 512
HEADS = 8
DH = 64
LAYERS = 2
NB = 32
BLOCK = 256
MICRO = 8
C = 1024


epsilon = 1e-05


def shards(
    candidates, key_cache, value_cache, w_in, w_out, rab_table, hist_len, hist_bucket, visible
):
    width = HEADS * DH
    factor = DH ** (-0.5)
    local_len = hist_len[0]
    hist_dev = key_cache.shape[1]
    width_local = key_cache.shape[2]
    heads_local = width_local // DH
    key_block = min(512, hist_dev)
    row_count = candidates.shape[0]
    visible_float = visible.astype(jnp.float32)
    stream = lax.all_gather(candidates, "hist", axis=0, tiled=True).astype(jnp.float32)
    for layer_index in range(LAYERS):
        project_average = jnp.mean(stream, axis=-1, keepdims=True)
        centred = stream - project_average
        variance = jnp.mean(centred * centred, axis=-1, keepdims=True)
        normed = (centred * lax.rsqrt(variance + epsilon)).astype(jnp.bfloat16)
        projected = jnp.dot(
            normed,
            w_in[layer_index].reshape(D, 4 * width_local),
            preferred_element_type=jnp.float32,
        )
        projected = jax.nn.silu(projected).astype(jnp.bfloat16).reshape(-1, 4, width_local)
        queries = projected[:, 0]
        keys_new = projected[:, 1]
        values_new = projected[:, 2]
        gates = projected[:, 3]
        one_hot = (hist_bucket[:, None] == jnp.arange(NB, dtype=jnp.int32)[None, :]).astype(
            jnp.float32
        )
        bias = jnp.dot(one_hot, rab_table[layer_index], precision=lax.Precision.HIGHEST)
        attend_query_count = queries.shape[0]
        micro_ids = jnp.arange(attend_query_count, dtype=jnp.int32) // (C // MICRO)
        picking = (micro_ids[:, None] == jnp.arange(MICRO, dtype=jnp.int32)[None, :]).astype(
            jnp.float32
        )
        visible_rows = jnp.dot(picking, visible_float, precision=lax.Precision.HIGHEST)
        attend_query_heads = queries.reshape(attend_query_count, heads_local, DH)
        cached_keys = key_cache[layer_index]
        cached_values = value_cache[layer_index]

        def block_step(block_index, summed):
            key_start = block_index * key_block

            def compute(held):
                key_part = lax.dynamic_slice_in_dim(cached_keys, key_start, key_block, 0).reshape(
                    key_block, heads_local, DH
                )
                value_part = lax.dynamic_slice_in_dim(
                    cached_values, key_start, key_block, 0
                ).reshape(key_block, heads_local, DH)
                bias_part = lax.dynamic_slice_in_dim(bias, key_start, key_block, 0)
                visible_part = lax.dynamic_slice_in_dim(
                    visible_rows, key_start // BLOCK, key_block // BLOCK, 1
                )
                positions = key_start + jnp.arange(key_block, dtype=jnp.int32)
                valid = (positions < local_len).astype(jnp.float32)
                masking = (
                    jnp.repeat(visible_part, BLOCK, axis=1, total_repeat_length=key_block)
                    * valid[None, :]
                )
                scores = jnp.einsum(
                    "rhd,khd->hrk", attend_query_heads, key_part, preferred_element_type=jnp.float32
                )
                scores = scores * factor + bias_part.T[:, None, :]
                weights = (jax.nn.silu(scores) * masking[None]).astype(jnp.bfloat16)
                return held + jnp.einsum(
                    "hrk,khd->rhd", weights, value_part, preferred_element_type=jnp.float32
                )

            return lax.cond(key_start < local_len, compute, lambda held: held, summed)

        summed = lax.fori_loop(
            0,
            hist_dev // key_block,
            block_step,
            jnp.zeros((attend_query_count, heads_local, DH), jnp.float32),
        )
        terms = summed.reshape(attend_query_count, width_local)
        attended = lax.psum(terms.astype(jnp.bfloat16), "hist").astype(jnp.float32)
        finish_attended = attended
        query_count = finish_attended.shape[0]
        query_heads = queries.astype(jnp.float32).reshape(query_count, heads_local, DH)
        key_heads = keys_new.astype(jnp.float32).reshape(query_count, heads_local, DH)
        value_heads = values_new.astype(jnp.float32).reshape(query_count, heads_local, DH)
        own_score = jax.nn.silu(jnp.sum(query_heads * key_heads, axis=-1) * factor)
        finish_attended = finish_attended + (own_score[..., None] * value_heads).reshape(
            query_count, width_local
        )
        totals = lax.psum(
            (
                jnp.sum(finish_attended, axis=-1),
                jnp.sum(finish_attended * finish_attended, axis=-1),
            ),
            "head",
        )
        average = (totals[0] / width)[:, None]
        squares = (totals[1] / width)[:, None]
        normalized = (finish_attended - average) * lax.rsqrt(squares - average * average + epsilon)
        gated = (normalized * gates.astype(jnp.float32)).astype(jnp.bfloat16)
        update = lax.psum(
            jnp.dot(gated, w_out[layer_index], preferred_element_type=jnp.float32).astype(
                jnp.bfloat16
            ),
            "head",
        ).astype(jnp.float32)
        stream = stream + update
    own_start = lax.axis_index("hist") * row_count
    return lax.dynamic_slice_in_dim(stream, own_start, row_count, 0).astype(jnp.bfloat16)


def solution(mesh):
    placed = (
        P(("users", "hist"), None),
        P(None, ("users", "hist"), "head"),
        P(None, ("users", "hist"), "head"),
        P(None, None, None, "head"),
        P(None, "head", None),
        P(None, None, "head"),
        P(("users", "hist")),
        P(("users", "hist")),
        P(None, ("users", "hist")),
    )
    return jax.shard_map(
        shards, mesh=mesh, in_specs=placed, out_specs=P(("users", "hist"), None), check_vma=False
    )
```

profile of v0, /device:TPU:0, one launch (start us, length us, event | category | flops | bytes accessed | tf_op | source)
XLA Modules:
  0.0 379.5 jit_solution(7019134319419471442)
XLA Ops:
  7.3 3.3 fusion.74
  10.6 1.2 copy.22
  13.6 1.5 copy.18
  16.8 1.5 copy.19
  19.4 33.2 %all-gather.2.cloned.1.call-done = bf16[1024,512]{1,0:T(8,128)(2,1)} async-done(((bf16[128,512]{1,0:T(8,128)(2,1)}), bf16[1024,512]{1,0:T(8,128)(2,1)}) %all-gather.2.cloned.1.call-update) | async-done | bytes 1048592 | tf_op jit(solution)/shard_map/all_gather | solution.py:31
  52.6 1.5 convert_reduce_fusion
  54.1 1.7 fusion.38
  55.9 2.6 multiply_convert_fusion.1
  58.5 1.3 copy-done.7
  62.0 52.3 %while.34 = (s32[]{:T(128)}, f32[1024,4,64]{0,2,1:T(8,128)}, s32[]{:T(128)}, bf16[2048,256]{0,1:T(8,128)(2,1)}, bf16[2048,256]{0,1:T(8,128)(2,1)}, /*index=5*/bf...) while((s32[]{:T(128)}, f32[1024,4,64]{0,2,1:T(8,128)}, ...), condition=%wide.region_5.7_spmd, body=%wide.region_2.6_spmd.sunk | while | flops 554437120 | bytes 14733740 | solution.py:92
  62.6 12.4 %conditional.4 = (f32[1024,4,64]{0,2,1:T(8,128)}) conditional(s32[]{:T(128)} %convert_element_type.273, f32[1024,4,64]{0,2,1:T(8,128)} %get-tuple-element.543, (s32[]{:T(128)}, bf16[2048,256]{0,1:T(8,128)(2,1)}, bf16[2048,256]{0,1:T(8,128)(2,1)}, bf16[1024,4,64]{0,2,1:T(8,128)(2,1)}, f32[2048,4]{0,1:T(4,128)S(1)}, /*index=5*/f32[1024,8]{0,1:T(8,128)S(1)}, ...), branch_computations={%region_3.3_spmd, %region_4.5_spmd} | conditional | flops 554437120 | bytes 14733549 | solution.py:90
  63.4 1.8 gather_fusion
  65.9 1.5 bitcast_multiply_fusion.1
  68.5 6.6 %fusion.12 = f32[1024,4,64]{0,2,1:T(8,128)} fusion(f32[1024,4,64]{0,2,1:T(8,128)} %get-tuple-element.336, bf16[512,4,64]{0,2,1:T(8,128)(2,1)S(1)} %bitcast.148, f32[1024,512]{0,1:T(8,128)} %bitcast_multiply_fusion.1, f32[4,512]{1,0:T(4,128)S(1)} %dynamic-slice_bitcast_fusion, bf16[512,4,64]{0,2,1:T(8,128)(2,1)S(1)} %bitcast.147, ...), kind=kOutput, calls=%fused_computation.13 | convolution fusion | flops 553910272 | bytes 5251072 | tf_op jit(solution)/shard_map/while/body/eval_jaxpr/cond/branch_1_fun/hrk,khd->rhd/dot_general | solution.py:86
  75.7 12.4 %conditional.4 = (f32[1024,4,64]{0,2,1:T(8,128)}) conditional(s32[]{:T(128)} %convert_element_type.273, f32[1024,4,64]{0,2,1:T(8,128)} %get-tuple-element.543, (s32[]{:T(128)}, bf16[2048,256]{0,1:T(8,128)(2,1)}, bf16[2048,256]{0,1:T(8,128)(2,1)}, bf16[1024,4,64]{0,2,1:T(8,128)(2,1)}, f32[2048,4]{0,1:T(4,128)S(1)}, /*index=5*/f32[1024,8]{0,1:T(8,128)S(1)}, ...), branch_computations={%region_3.3_spmd, %region_4.5_spmd} | conditional | flops 554437120 | bytes 14733549 | solution.py:90
  76.4 1.8 gather_fusion
  78.9 1.5 bitcast_multiply_fusion.1
  81.5 6.6 %fusion.12 = f32[1024,4,64]{0,2,1:T(8,128)} fusion(f32[1024,4,64]{0,2,1:T(8,128)} %get-tuple-element.336, bf16[512,4,64]{0,2,1:T(8,128)(2,1)S(1)} %bitcast.148, f32[1024,512]{0,1:T(8,128)} %bitcast_multiply_fusion.1, f32[4,512]{1,0:T(4,128)S(1)} %dynamic-slice_bitcast_fusion, bf16[512,4,64]{0,2,1:T(8,128)(2,1)S(1)} %bitcast.147, ...), kind=kOutput, calls=%fused_computation.13 | convolution fusion | flops 553910272 | bytes 5251072 | tf_op jit(solution)/shard_map/while/body/eval_jaxpr/cond/branch_1_fun/hrk,khd->rhd/dot_general | solution.py:86
  88.8 12.4 %conditional.4 = (f32[1024,4,64]{0,2,1:T(8,128)}) conditional(s32[]{:T(128)} %convert_element_type.273, f32[1024,4,64]{0,2,1:T(8,128)} %get-tuple-element.543, (s32[]{:T(128)}, bf16[2048,256]{0,1:T(8,128)(2,1)}, bf16[2048,256]{0,1:T(8,128)(2,1)}, bf16[1024,4,64]{0,2,1:T(8,128)(2,1)}, f32[2048,4]{0,1:T(4,128)S(1)}, /*index=5*/f32[1024,8]{0,1:T(8,128)S(1)}, ...), branch_computations={%region_3.3_spmd, %region_4.5_spmd} | conditional | flops 554437120 | bytes 14733549 | solution.py:90
  89.5 1.8 gather_fusion
  92.0 1.5 bitcast_multiply_fusion.1
  94.6 6.6 %fusion.12 = f32[1024,4,64]{0,2,1:T(8,128)} fusion(f32[1024,4,64]{0,2,1:T(8,128)} %get-tuple-element.336, bf16[512,4,64]{0,2,1:T(8,128)(2,1)S(1)} %bitcast.148, f32[1024,512]{0,1:T(8,128)} %bitcast_multiply_fusion.1, f32[4,512]{1,0:T(4,128)S(1)} %dynamic-slice_bitcast_fusion, bf16[512,4,64]{0,2,1:T(8,128)(2,1)S(1)} %bitcast.147, ...), kind=kOutput, calls=%fused_computation.13 | convolution fusion | flops 553910272 | bytes 5251072 | tf_op jit(solution)/shard_map/while/body/eval_jaxpr/cond/branch_1_fun/hrk,khd->rhd/dot_general | solution.py:86
  101.8 12.4 %conditional.4 = (f32[1024,4,64]{0,2,1:T(8,128)}) conditional(s32[]{:T(128)} %convert_element_type.273, f32[1024,4,64]{0,2,1:T(8,128)} %get-tuple-element.543, (s32[]{:T(128)}, bf16[2048,256]{0,1:T(8,128)(2,1)}, bf16[2048,256]{0,1:T(8,128)(2,1)}, bf16[1024,4,64]{0,2,1:T(8,128)(2,1)}, f32[2048,4]{0,1:T(4,128)S(1)}, /*index=5*/f32[1024,8]{0,1:T(8,128)S(1)}, ...), branch_computations={%region_3.3_spmd, %region_4.5_spmd} | conditional | flops 554437120 | bytes 14733549 | solution.py:90
  102.6 1.8 gather_fusion
  105.1 1.5 bitcast_multiply_fusion.1
  107.7 6.6 %fusion.12 = f32[1024,4,64]{0,2,1:T(8,128)} fusion(f32[1024,4,64]{0,2,1:T(8,128)} %get-tuple-element.336, bf16[512,4,64]{0,2,1:T(8,128)(2,1)S(1)} %bitcast.148, f32[1024,512]{0,1:T(8,128)} %bitcast_multiply_fusion.1, f32[4,512]{1,0:T(4,128)S(1)} %dynamic-slice_bitcast_fusion, bf16[512,4,64]{0,2,1:T(8,128)(2,1)S(1)} %bitcast.147, ...), kind=kOutput, calls=%fused_computation.13 | convolution fusion | flops 553910272 | bytes 5251072 | tf_op jit(solution)/shard_map/while/body/eval_jaxpr/cond/branch_1_fun/hrk,khd->rhd/dot_general | solution.py:86
  114.3 2.2 convert_element_type.165
  116.8 71.2 %all-reduce.7.cloned.1.call-done = bf16[1024,256]{0,1:T(8,128)(2,1)} async-done(((bf16[1024,256]{0,1:T(8,128)(2,1)}), bf16[1024,256]{0,1:T(8,128)(2,1)}) %all-reduce.7.cloned.1.call-update) | async-done | bytes 524304 | tf_op jit(solution)/shard_map/psum | solution.py:99
  188.0 1.5 fusion.53
  189.5 2.5 all-reduce.1
  192.0 1.8 fusion.44
  193.8 2.5 convolution_convert_fusion.1
  197.8 1.4 copy.20
  199.2 1.5 copy.21
  201.4 13.7 %all-reduce.9.cloned.1.call-done = bf16[1024,512]{1,0:T(8,128)(2,1)} async-done(((bf16[1024,512]{1,0:T(8,128)(2,1)}), bf16[1024,512]{1,0:T(8,128)(2,1)}) %all-reduce.9.cloned.1.call-update) | async-done | bytes 1048592 | tf_op jit(solution)/shard_map/psum | solution.py:120
  215.1 1.7 fusion.72
  216.7 1.8 multiply_reduce_fusion
  218.6 2.7 multiply_convert_fusion
  221.3 1.2 fusion.73
  223.1 47.8 %while.35 = (s32[]{:T(128)}, f32[1024,4,64]{0,2,1:T(8,128)S(1)}, s32[]{:T(128)}, bf16[2048,256]{0,1:T(8,128)(2,1)}, bf16[2048,256]{0,1:T(8,128)(2,1)}, /*index=5...) while((s32[]{:T(128)}, f32[1024,4,64]{0,2,1:T(8,128)S(1)}, ...), condition=%wide.region_18.20_spmd, body=%wide.region_15.19_spmd.sunk | while | flops 554437120 | bytes 14733740 | solution.py:92
  223.8 11.3 %conditional.5 = (f32[1024,4,64]{0,2,1:T(8,128)S(1)}) conditional(s32[]{:T(128)} %convert_element_type.274, f32[1024,4,64]{0,2,1:T(8,128)S(1)} %get-tuple-element.573, (s32[]{:T(128)}, bf16[2048,256]{0,1:T(8,128)(2,1)}, bf16[2048,256]{0,1:T(8,128)(2,1)}, bf16[1024,4,64]{0,2,1:T(8,128)(2,1)}, f32[2048,4]{0,1:T(4,128)S(1)}, ...), branch_computations={%region_16.17_spmd, %region_17.18_spmd} | conditional | flops 554437120 | bytes 14733549 | solution.py:90
  224.5 1.8 gather_fusion.1
  227.0 1.5 bitcast_multiply_fusion.3
  229.6 5.4 %fusion.30 = f32[1024,4,64]{0,2,1:T(8,128)S(1)} fusion(f32[1024,4,64]{0,2,1:T(8,128)S(1)} %get-tuple-element.353, bf16[512,4,64]{0,2,1:T(8,128)(2,1)S(1)} %bitcast.150, f32[1024,512]{0,1:T(8,128)} %bitcast_multiply_fusion.3, f32[4,512]{1,0:T(4,128)S(1)} %dynamic-slice_bitcast_fusion.1, bf16[512,4,64]{0,2,1:T(8,128)(2,1)S(1)} %bitcast.149, ...), kind=kOutput, calls=%fused_computation.34 | convolution fusion | flops 553910272 | bytes 5251072 | tf_op jit(solution)/shard_map/while/body/eval_jaxpr/cond/branch_1_fun/hrk,khd->rhd/dot_general | solution.py:86
  235.7 11.3 %conditional.5 = (f32[1024,4,64]{0,2,1:T(8,128)S(1)}) conditional(s32[]{:T(128)} %convert_element_type.274, f32[1024,4,64]{0,2,1:T(8,128)S(1)} %get-tuple-element.573, (s32[]{:T(128)}, bf16[2048,256]{0,1:T(8,128)(2,1)}, bf16[2048,256]{0,1:T(8,128)(2,1)}, bf16[1024,4,64]{0,2,1:T(8,128)(2,1)}, f32[2048,4]{0,1:T(4,128)S(1)}, ...), branch_computations={%region_16.17_spmd, %region_17.18_spmd} | conditional | flops 554437120 | bytes 14733549 | solution.py:90
  236.5 1.8 gather_fusion.1
  239.0 1.5 bitcast_multiply_fusion.3
  241.6 5.4 %fusion.30 = f32[1024,4,64]{0,2,1:T(8,128)S(1)} fusion(f32[1024,4,64]{0,2,1:T(8,128)S(1)} %get-tuple-element.353, bf16[512,4,64]{0,2,1:T(8,128)(2,1)S(1)} %bitcast.150, f32[1024,512]{0,1:T(8,128)} %bitcast_multiply_fusion.3, f32[4,512]{1,0:T(4,128)S(1)} %dynamic-slice_bitcast_fusion.1, bf16[512,4,64]{0,2,1:T(8,128)(2,1)S(1)} %bitcast.149, ...), kind=kOutput, calls=%fused_computation.34 | convolution fusion | flops 553910272 | bytes 5251072 | tf_op jit(solution)/shard_map/while/body/eval_jaxpr/cond/branch_1_fun/hrk,khd->rhd/dot_general | solution.py:86
  247.7 11.3 %conditional.5 = (f32[1024,4,64]{0,2,1:T(8,128)S(1)}) conditional(s32[]{:T(128)} %convert_element_type.274, f32[1024,4,64]{0,2,1:T(8,128)S(1)} %get-tuple-element.573, (s32[]{:T(128)}, bf16[2048,256]{0,1:T(8,128)(2,1)}, bf16[2048,256]{0,1:T(8,128)(2,1)}, bf16[1024,4,64]{0,2,1:T(8,128)(2,1)}, f32[2048,4]{0,1:T(4,128)S(1)}, ...), branch_computations={%region_16.17_spmd, %region_17.18_spmd} | conditional | flops 554437120 | bytes 14733549 | solution.py:90
  248.4 1.8 gather_fusion.1
  250.9 1.5 bitcast_multiply_fusion.3
  253.5 5.4 %fusion.30 = f32[1024,4,64]{0,2,1:T(8,128)S(1)} fusion(f32[1024,4,64]{0,2,1:T(8,128)S(1)} %get-tuple-element.353, bf16[512,4,64]{0,2,1:T(8,128)(2,1)S(1)} %bitcast.150, f32[1024,512]{0,1:T(8,128)} %bitcast_multiply_fusion.3, f32[4,512]{1,0:T(4,128)S(1)} %dynamic-slice_bitcast_fusion.1, bf16[512,4,64]{0,2,1:T(8,128)(2,1)S(1)} %bitcast.149, ...), kind=kOutput, calls=%fused_computation.34 | convolution fusion | flops 553910272 | bytes 5251072 | tf_op jit(solution)/shard_map/while/body/eval_jaxpr/cond/branch_1_fun/hrk,khd->rhd/dot_general | solution.py:86
  259.6 11.3 %conditional.5 = (f32[1024,4,64]{0,2,1:T(8,128)S(1)}) conditional(s32[]{:T(128)} %convert_element_type.274, f32[1024,4,64]{0,2,1:T(8,128)S(1)} %get-tuple-element.573, (s32[]{:T(128)}, bf16[2048,256]{0,1:T(8,128)(2,1)}, bf16[2048,256]{0,1:T(8,128)(2,1)}, bf16[1024,4,64]{0,2,1:T(8,128)(2,1)}, f32[2048,4]{0,1:T(4,128)S(1)}, ...), branch_computations={%region_16.17_spmd, %region_17.18_spmd} | conditional | flops 554437120 | bytes 14733549 | solution.py:90
  260.4 1.8 gather_fusion.1
  262.9 1.5 bitcast_multiply_fusion.3
  265.5 5.4 %fusion.30 = f32[1024,4,64]{0,2,1:T(8,128)S(1)} fusion(f32[1024,4,64]{0,2,1:T(8,128)S(1)} %get-tuple-element.353, bf16[512,4,64]{0,2,1:T(8,128)(2,1)S(1)} %bitcast.150, f32[1024,512]{0,1:T(8,128)} %bitcast_multiply_fusion.3, f32[4,512]{1,0:T(4,128)S(1)} %dynamic-slice_bitcast_fusion.1, bf16[512,4,64]{0,2,1:T(8,128)(2,1)S(1)} %bitcast.149, ...), kind=kOutput, calls=%fused_computation.34 | convolution fusion | flops 553910272 | bytes 5251072 | tf_op jit(solution)/shard_map/while/body/eval_jaxpr/cond/branch_1_fun/hrk,khd->rhd/dot_general | solution.py:86
  271.9 1.4 fusion.43
  273.4 72.6 %all-reduce.11.cloned.1.call-done = bf16[1024,256]{0,1:T(8,128)(2,1)} async-done(((bf16[1024,256]{0,1:T(8,128)(2,1)}), bf16[1024,256]{0,1:T(8,128)(2,1)}) %all-reduce.11.cloned.1.call-update) | async-done | bytes 524304 | tf_op jit(solution)/shard_map/psum | solution.py:99
  345.9 1.3 fusion.54
  347.2 2.5 all-reduce
  349.7 1.4 fusion.41
  351.1 1.5 convolution_convert_fusion
  352.6 18.7 %all-reduce.13.cloned.1.call-done = bf16[1024,512]{1,0:T(8,128)(2,1)} async-done(((bf16[1024,512]{1,0:T(8,128)(2,1)}), bf16[1024,512]{1,0:T(8,128)(2,1)}) %all-reduce.13.cloned.1.call-update) | async-done | bytes 1048592 | tf_op jit(solution)/shard_map/psum | solution.py:120
  371.3 1.7 fusion.58
  (105 shorter events, 31.1 us)
Async XLA Ops:
  6.5 46.1 %all-gather.2.cloned.1.call-start = ((), (), s32[]{:S(2)}) async-start(), calls=%async_computation | async-start | bytes 1179648 | tf_op jit(solution)/shard_map/all_gather | solution.py:31
  7.3 180.7 %all-reduce.7.cloned.1.call-start = ((), (), s32[]{:S(2)}) async-start(), calls=%async_computation.1 | async-start | bytes 1048576 | tf_op jit(solution)/shard_map/psum | solution.py:99
  10.6 2.0 copy-start.8
  13.6 2.0 copy-start.9
  16.7 1.5 copy-start.16
  16.8 1.9 copy-start.15
  16.8 2.0 copy-start.17
  16.8 39.1 %copy-start.12 = (bf16[64,8,4,256]{3,1,2,0:T(8,128)(2,1)S(1)}, bf16[64,8,4,256]{3,1,2,0:T(8,128)(2,1)}, u32[]{:S(2)}) copy-start(bf16[64,8,4,256]{3,1,2,0:T(8,128)(2,1)} %copy.22) | copy-start | bytes 3145732
  52.6 3.3 copy-start
  58.5 1.3 copy-start.7
  114.3 2.3 copy-start.10
  114.3 2.3 copy-start.11
  116.5 98.6 %all-reduce.9.cloned.1.call-start = ((), (), s32[]{:S(2)}) async-start(), calls=%async_computation.2 | async-start | bytes 2097152 | tf_op jit(solution)/shard_map/psum | solution.py:120
  192.0 4.6 %copy-start.1 = (bf16[1,512,4,256]{3,2,1,0:T(4,128)(2,1)S(1)}, bf16[1,512,4,256]{3,2,1,0:T(4,128)(2,1)}, u32[]{:S(2)}) copy-start(bf16[1,512,4,256]{3,2,1,0:T(4,128)(2,1)} %get-tuple-element.422) | copy-start | bytes 3145732
  193.7 4.0 %copy-start.2 = (bf16[1,2048,256]{2,1,0:T(8,128)(2,1)S(1)}, bf16[1,2048,256]{2,1,0:T(8,128)(2,1)}, u32[]{:S(2)}) copy-start(bf16[1,2048,256]{2,1,0:T(8,128)(2,1)} %get-tuple-element.426) | copy-start | bytes 3145732
  196.3 149.6 %all-reduce.11.cloned.1.call-start = ((), (), s32[]{:S(2)}) async-start(), calls=%async_computation.3 | async-start | bytes 1048576 | tf_op jit(solution)/shard_map/psum | solution.py:99
  197.8 1.4 copy-start.3
  215.1 1.7 copy-start.4
  216.7 1.9 copy-start.13
  221.2 1.7 copy-start.5
  270.9 75.0 %copy-start.6 = (bf16[1024,1024]{0,1:T(8,128)(2,1)S(1)}, bf16[1024,1024]{0,1:T(8,128)(2,1)}, u32[]{:S(2)}) copy-start(bf16[1024,1024]{0,1:T(8,128)(2,1)} %copy-done.5) | copy-start | bytes 6291460
  271.8 99.5 %all-reduce.13.cloned.1.call-start = ((), (), s32[]{:S(2)}) async-start(), calls=%async_computation.4 | async-start | bytes 2097152 | tf_op jit(solution)/shard_map/psum | solution.py:120
  271.9 79.2 %copy-start.14 = (bf16[2,256,512]{2,1,0:T(8,128)(2,1)S(1)}, bf16[2,256,512]{2,1,0:T(8,128)(2,1)}, u32[]{:S(2)}) copy-start(bf16[2,256,512]{2,1,0:T(8,128)(2,1)} %param.27) | copy-start | bytes 1572868
Sparse Core Ops, SparseCore 0:
  9.5 43.0 all-gather.1
  116.6 71.3 all-reduce.6
  196.4 18.5 all-reduce.8
  271.9 73.9 all-reduce.10
  352.7 18.5 all-reduce.12
where the time goes:
time: 379 us; the launch traced here: 380 us
  waiting for transfers between devices  210 us (55%)
  matrix products  59.1 us (16%)
  local copies, waits for them, and re-layouts  43.8 us (12%)
  other arithmetic  41.9 us (11%)
  between operations  13.4 us (4%)
  loops' own time  5.95 us (2%)
  blocking collectives  4.99 us (1%)
    psum x2, waiting for transfers between devices, shards(): attended = lax.psum(terms.astype(jnp.bfloat16), 'hist').astype(jnp.float32)  144 us
    dot_general x8, matrix products, compute(): jnp.einsum('hrk,khd->rhd', weights, value_part, preferred_element_type=jn...  47.9 us
    all_gather x1, waiting for transfers between devices, shards(): lax.all_gather(candidates, 'hist', axis=0, tiled=True).astype(jnp.float32)  33.2 us
    psum x2, waiting for transfers between devices, shards(): lax.psum(jnp.dot(gated, w_out[layer_index], preferred_element_type=jnp.fl...  32.4 us
    gather x8, local copies, waits for them, and re-layouts, compute(): jnp.repeat(visible_part, BLOCK, axis=1, total_repeat_length=key_block)  14.7 us
    mul x8, other arithmetic, compute(): jnp.repeat(visible_part, BLOCK, axis=1, total_repeat_length=key_block)  12.1 us
    unnamed x42, local copies, waits for them, and re-layouts  11.4 us
    dynamic_slice x8, local copies, waits for them, and re-layouts, compute(): lax.dynamic_slice_in_dim(cached_keys, key_start, key_block, 0)  8.52 us
  transfers between devices with their start and end apart: 5, of which 5 were waited for; matrix products, arithmetic and copies ran while one was open for 5% of the time, Pallas kernels for 0%

commit v1 on v0

v1 whole, which is shorter than its diff:
```python
import functools
import jax
import jax.numpy as jnp
from jax import lax
from jax.experimental import pallas as pl
from jax.experimental.pallas import tpu as pltpu
from jax.sharding import PartitionSpec as P

epsilon = 1e-05
LANES = 128
F32, BF16 = jnp.float32, jnp.bfloat16
NT = (((1,), (1,)), ((), ()))
NN = (((1,), (0,)), ((), ()))
SMEM = pl.BlockSpec(memory_space=pltpu.SMEM)
VMEM = pl.BlockSpec(memory_space=pltpu.VMEM)


def half_silu(y):
    return y + y * jnp.tanh(y)


def norm_rows(x):
    mean = jnp.mean(x, axis=-1, keepdims=True)
    centred = x - mean
    variance = jnp.mean(centred * centred, axis=-1, keepdims=True)
    return (centred * lax.rsqrt(variance + epsilon)).astype(BF16)


def mm(a, b, dims=NN):
    return lax.dot_general(a, b, dims, preferred_element_type=F32)


def first_kernel(x_ref, w_ref, normed_ref, q_ref):
    normed = norm_rows(x_ref[...].astype(F32))
    normed_ref[...] = normed
    q_ref[...] = half_silu(0.5 * mm(normed, w_ref[...])).astype(BF16)


def rest_kernel(dh, normed_ref, q_ref, wk_ref, wv_ref, wg_ref, own_ref, gate_ref):
    normed = normed_ref[...]
    part = lambda w: half_silu(0.5 * mm(normed, w[...])).astype(BF16)
    product = q_ref[...].astype(F32) * part(wk_ref).astype(F32)
    head = lax.broadcasted_iota(jnp.int32, product.shape, 1) // dh
    score = jnp.zeros_like(product)
    for h in range(product.shape[1] // dh):
        total = jnp.sum(jnp.where(head == h, product, 0.0), axis=-1, keepdims=True)
        score = jnp.where(head == h, half_silu(total * (0.5 * dh**-0.5)), score)
    own_ref[...] = score * part(wv_ref).astype(F32)
    gate_ref[...] = part(wg_ref).astype(F32)


def index_kernel(micro, nblk, block, nb, len_ref, vis_ref, bucket_ref, oh_ref, list_ref):
    count = len_ref[0]
    for m in range(micro):

        def step(b, filled):
            list_ref[m, 1 + filled] = b
            ok = jnp.logical_and(vis_ref[m, b] != 0, b * block < count)
            return filled + jnp.where(ok, 1, 0)

        filled = lax.fori_loop(0, nblk, step, jnp.int32(0))
        list_ref[m, 0] = filled
        list_ref[m, 1 + filled] = nblk
    row = lax.broadcasted_iota(jnp.int32, (LANES, block), 0)
    for b in range(nblk):
        bucket = jnp.broadcast_to(bucket_ref[b : b + 1, :], (LANES, block))
        hit = jnp.logical_and(bucket == row % nb, row < 3 * nb)
        oh_ref[b * block : (b + 1) * block, :] = jnp.where(hit, 1.0, 0.0).T.astype(BF16)


def turn_kernel(nblk, block, len_ref, v_ref, vt_ref):
    count = len_ref[0]
    width = v_ref.shape[1]
    lane = lax.broadcasted_iota(jnp.int32, (width, block), 1)
    for b in range(nblk):
        turned = v_ref[b * block : (b + 1) * block, :].astype(F32).T
        vt_ref[b] = jnp.where(lane + b * block < count, turned, 0.0).astype(BF16)
    vt_ref[nblk] = jnp.zeros((width, block), BF16)


def attend_kernel(pieces, unit, nblk, block, nb, dh, order_ref, list_ref, rab_ref, k_ref, oh_ref, vt_ref, *rest):
    q_refs, out_refs = rest[:pieces], rest[pieces : 2 * pieces]
    w_ref, acc_ref = rest[2 * pieces :]
    heads = acc_ref.shape[1] // dh
    pair_width = 2 * dh
    per = q_refs[0].shape[0] // unit
    lane = lax.broadcasted_iota(jnp.int32, rab_ref.shape, 1)
    bias = 0.5 * rab_ref[...]
    high = bias.astype(BF16).astype(F32)
    mid = (bias - high).astype(BF16).astype(F32)
    low = bias - high - mid
    bias = jnp.where(lane < nb, high, jnp.where(lane < 2 * nb, mid, jnp.where(lane < 3 * nb, low, 0.0)))
    qlane = lax.broadcasted_iota(jnp.int32, (unit, pair_width), 1)
    for p in range(pieces):
        for u in range(per):
            slot = p * per + u
            rows = q_refs[p][u * unit : (u + 1) * unit, :].astype(F32) * (0.5 * dh**-0.5)
            for pair in range(heads // 2):
                part = rows[:, pair * pair_width : (pair + 1) * pair_width]
                for h in range(2):
                    mine = jnp.logical_and(qlane >= h * dh, qlane < (h + 1) * dh)
                    span = slice(h * unit, (h + 1) * unit)
                    w_ref[slot, pair, span, 0:pair_width] = jnp.where(mine, part, 0.0).astype(BF16)
                    head = 2 * pair + h
                    w_ref[slot, pair, span, pair_width:] = jnp.broadcast_to(
                        bias[head : head + 1, :], (unit, LANES)
                    ).astype(BF16)

    def one(slot, carry):
        m = order_ref[slot]
        acc_ref[slot] = jnp.zeros(acc_ref.shape[1:], F32)

        def two_blocks(t, inner):
            sums = [None] * heads
            for j in range(2):
                b = list_ref[m, 1 + 2 * t + j]
                start = pl.multiple_of(jnp.where(b == nblk, 0, b) * block, block)
                hot = oh_ref[pl.ds(start, block), :]
                for pair in range(heads // 2):
                    keys = k_ref[pl.ds(start, block), pair * pair_width : (pair + 1) * pair_width]
                    y = mm(jnp.concatenate([keys, hot], axis=1), w_ref[slot, pair], NT)
                    weights = half_silu(y).astype(BF16)
                    for h in range(2):
                        head = 2 * pair + h
                        values = vt_ref[b, head * dh : (head + 1) * dh, :]
                        term = mm(values, weights[:, h * unit : (h + 1) * unit])
                        sums[head] = term if j == 0 else sums[head] + term
            for head in range(heads):
                acc_ref[slot, head * dh : (head + 1) * dh, :] += sums[head]
            return inner

        lax.fori_loop(0, (list_ref[m, 0] + 1) // 2, two_blocks, 0)
        return carry

    lax.fori_loop(0, pieces * per, one, 0)
    for p in range(pieces):
        for u in range(per):
            out_refs[p][u * unit : (u + 1) * unit, :] = acc_ref[p * per + u].T.astype(BF16)


def combine_kernel(*refs):
    *parts, own_ref, gate_ref, out_ref = refs
    total = own_ref[...]
    for part in parts:
        total = total + part[...].astype(F32)
    width = total.shape[1]
    out_ref[:, :width] = total
    out_ref[:, width:] = gate_ref[...]


def finish_kernel(last, head_ref, mine_ref, other_ref, wa_ref, wb_ref, stream_ref, *rest):
    lead = head_ref[0] == 0
    width = mine_ref.shape[1] // 2
    mine, other = mine_ref[...], other_ref[...]
    first, second = jnp.where(lead, mine, other), jnp.where(lead, other, mine)
    att = [first[:, :width], second[:, :width]]
    gates = [first[:, width:], second[:, width:]]
    total = sum(jnp.sum(a, axis=-1, keepdims=True) for a in att) / (2 * width)
    square = sum(jnp.sum(a * a, axis=-1, keepdims=True) for a in att) / (2 * width)
    scale = lax.rsqrt(square - total * total + epsilon)
    gated = [((a - total) * scale * g).astype(BF16) for a, g in zip(att, gates)]
    wa, wb = wa_ref[...], wb_ref[...]
    update = mm(gated[0], jnp.where(lead, wa, wb)) + mm(gated[1], jnp.where(lead, wb, wa))
    stream = stream_ref[...].astype(F32) + update
    if last:
        (out_ref,) = rest
        out_ref[...] = stream.astype(BF16)
        return
    w_ref, out_ref, normed_ref, q_ref = rest
    out_ref[...] = stream
    normed = norm_rows(stream)
    normed_ref[...] = normed
    q_ref[...] = half_silu(0.5 * mm(normed, w_ref[...])).astype(BF16)


def struct(shape, kind):
    return jax.ShapeDtypeStruct(shape, kind)


def layer_of(index, array):
    shape = array.shape[1:]
    return pl.BlockSpec((None,) + shape, lambda i: (index,) + (0,) * len(shape))


def whole(array):
    return pl.BlockSpec(array.shape, lambda i: (0,) * len(array.shape))


def cost(flops, size):
    return pl.CostEstimate(flops=flops, bytes_accessed=size, transcendentals=0)


def shards(n, candidates, key_cache, value_cache, w_in, w_out, rab_table, hist_len, hist_bucket, visible):
    layers, hist_dev, width = key_cache.shape
    heads = rab_table.shape[2]
    nb = rab_table.shape[1]
    dh = width // heads
    micro, nblk = visible.shape
    block = hist_dev // nblk
    rows, d = candidates.shape
    unit = rows * n // micro
    me = lax.axis_index("hist")
    head = lax.axis_index("head").reshape(1)
    direct = rows % unit == 0

    oh, lists = pl.pallas_call(
        functools.partial(index_kernel, micro, nblk, block, nb),
        out_shape=(struct((hist_dev, LANES), BF16), struct((micro, nblk + 2), jnp.int32)),
        in_specs=[SMEM, SMEM, VMEM],
        out_specs=(VMEM, SMEM),
        cost_estimate=cost(10**8, 10**6),
    )(hist_len, visible, hist_bucket.reshape(nblk, block))

    def turned(layer):
        return pl.pallas_call(
            functools.partial(turn_kernel, nblk, block),
            grid=(1,),
            out_shape=struct((nblk + 1, width, block), BF16),
            in_specs=[SMEM, layer_of(layer, value_cache)],
            out_specs=pl.BlockSpec((nblk + 1, width, block), lambda i: (0, 0, 0)),
            cost_estimate=cost(10**8, 2 * 10**6),
        )(hist_len, value_cache)

    def attend(layer, pieces, order, vt):
        units = len(pieces) * pieces[0].shape[0] // unit
        rab = jnp.tile(rab_table[layer].T, (1, LANES // nb))
        return pl.pallas_call(
            functools.partial(attend_kernel, len(pieces), unit, nblk, block, nb, dh),
            grid=(1,),
            out_shape=[struct(p.shape, BF16) for p in pieces],
            in_specs=[SMEM, SMEM, whole(rab), layer_of(layer, key_cache), whole(oh), whole(vt)]
            + [whole(p) for p in pieces],
            out_specs=[whole(p) for p in pieces],
            scratch_shapes=[
                pltpu.VMEM((units, heads // 2, 2 * unit, 2 * LANES), BF16),
                pltpu.VMEM((units, width, unit), F32),
            ],
            compiler_params=pltpu.CompilerParams(vmem_limit_bytes=32 << 20),
            cost_estimate=cost(10**10, 4 * 10**6),
        )(order, lists, rab, key_cache, oh, vt, *pieces)

    def swap(x, k):
        return lax.ppermute(x, "hist", [(i, i ^ k) for i in range(n)])

    swap_heads = lambda x: lax.ppermute(x, "head", [(0, 1), (1, 0)])
    weights = [[w_in[layer, :, j] for j in range(4)] for layer in range(layers)]
    w_other = swap_heads(w_out)
    normed, q = pl.pallas_call(
        first_kernel,
        out_shape=(struct((rows, d), BF16), struct((rows, width), BF16)),
        cost_estimate=cost(10**8, 10**6),
    )(candidates, weights[0][0])
    stream = candidates
    for layer in range(layers):
        if direct:
            pieces = [q] + [swap(q, k) for k in range(1, n)]
            order = me ^ jnp.arange(n, dtype=jnp.int32)
            order = (order[:, None] * (rows // unit) + jnp.arange(rows // unit, dtype=jnp.int32)).reshape(-1)
        else:
            pieces = [lax.all_gather(q, "hist", axis=0, tiled=True)]
            order = jnp.arange(micro, dtype=jnp.int32)
        own, gates = pl.pallas_call(
            functools.partial(rest_kernel, dh),
            out_shape=(struct((rows, width), F32),) * 2,
            cost_estimate=cost(10**8, 10**6),
        )(normed, q, *weights[layer][1:])
        vt = turned(layer)
        outs = attend(layer, pieces, order, vt)
        if direct:
            parts = [outs[0]] + [swap(outs[k], k) for k in range(1, n)]
        else:
            moved = lax.all_to_all(outs[0].reshape(n, rows, width), "hist", 0, 0)
            parts = [moved[i] for i in range(n)]
        mine = pl.pallas_call(
            combine_kernel,
            out_shape=struct((rows, 2 * width), F32),
            cost_estimate=cost(10**6, 10**6),
        )(*parts, own, gates)
        other = swap_heads(mine)
        last = layer == layers - 1
        common = [whole(mine), whole(other), layer_of(layer, w_out), layer_of(layer, w_out), whole(stream)]
        if last:
            return pl.pallas_call(
                functools.partial(finish_kernel, True),
                grid=(1,),
                out_shape=struct((rows, d), BF16),
                in_specs=[SMEM] + common,
                out_specs=whole(stream),
                cost_estimate=cost(10**8, 10**6),
            )(head, mine, other, w_out, w_other, stream)
        outs = (struct((rows, d), F32), struct((rows, d), BF16), struct((rows, width), BF16))
        stream, normed, q = pl.pallas_call(
            functools.partial(finish_kernel, False),
            grid=(1,),
            out_shape=outs,
            in_specs=[SMEM] + common + [whole(weights[layer + 1][0])],
            out_specs=tuple(whole(o) for o in outs),
            cost_estimate=cost(10**8, 10**6),
        )(head, mine, other, w_out, w_other, stream, weights[layer + 1][0])


def solution(mesh):
    placed = (
        P(("users", "hist"), None),
        P(None, ("users", "hist"), "head"),
        P(None, ("users", "hist"), "head"),
        P(None, None, None, "head"),
        P(None, "head", None),
        P(None, None, "head"),
        P(("users", "hist")),
        P(("users", "hist")),
        P(None, ("users", "hist")),
    )
    return jax.shard_map(
        functools.partial(shards, mesh.shape["hist"]),
        mesh=mesh,
        in_specs=placed,
        out_specs=P(("users", "hist"), None),
        check_vma=False,
    )
```

time: 379 us -> 140 us (0.37)
  waiting for transfers between devices: 210 us -> 14.6 us
  starting transfers between devices: 0.35 us -> 68.2 us
  matrix products: 59.1 us -> 0 us
  other arithmetic: 41.9 us -> 0.01 us
  Pallas kernels: 0 us -> 31.5 us
  local copies, waits for them, and re-layouts: 43.8 us -> 23.1 us
  between operations: 13.4 us -> 0.95 us
  loops' own time: 5.95 us -> 0 us
  blocking collectives: 4.99 us -> 0 us
    psum x4 -> x0, waiting for transfers between devices: 176 us -> none  [the longest x2 144 us: shards(): attended = lax.psum(terms.astype(jnp.bfloat16), 'hist').astype(jnp.float32)]
    ppermute x0 -> x31, starting transfers between devices: none -> 68.2 us  [the longest x28 68.2 us: swap(): return lax.ppermute(x, 'hist', [(i, i ^ k) for i in range(n)])]
    dot_general x15 -> x0, matrix products: 59.1 us -> none  [the longest x8 47.9 us: compute(): jnp.einsum('hrk,khd->rhd', weights, value_part, preferred_element_type=jn...]
    all_gather x1 -> x0, waiting for transfers between devices: 33.2 us -> none  [shards(): lax.all_gather(candidates, 'hist', axis=0, tiled=True).astype(jnp.float32)]
    pallas_call x0 -> x12, Pallas kernels: none -> 31.5 us  [the longest x2 8.38 us: attend(): pl.pallas_call(functools.partial(attend_kernel, len(pieces), unit, nblk,...]
    gather x8 -> x0, local copies, waits for them, and re-layouts: 14.7 us -> none  [compute(): jnp.repeat(visible_part, BLOCK, axis=1, total_repeat_length=key_block)]
    ppermute x0 -> x31, waiting for transfers between devices: none -> 14.6 us  [the longest x28 12.9 us: swap(): return lax.ppermute(x, 'hist', [(i, i ^ k) for i in range(n)])]
    convert_element_type x13 -> x0, other arithmetic: 13.1 us -> none  [the longest x8 5.21 us: compute(): valid = (positions < local_len).astype(jnp.float32)]
  transfers between devices with their start and end apart: 5 -> 31, of which waited for: 5 -> 8; matrix products, arithmetic and copies ran while one was open for 5% -> 4% of each run, Pallas kernels for 0% -> 10%
where the time goes in v1:
time: 140 us; the launch traced here: 138 us
  starting transfers between devices  68.2 us (49%)
  Pallas kernels  31.5 us (22%)
  local copies, waits for them, and re-layouts  23.1 us (16%)
  waiting for transfers between devices  14.6 us (10%)
    ppermute x28, starting transfers between devices, swap(): return lax.ppermute(x, 'hist', [(i, i ^ k) for i in range(n)])  68.2 us
    ppermute x28, waiting for transfers between devices, swap(): return lax.ppermute(x, 'hist', [(i, i ^ k) for i in range(n)])  12.9 us
    unnamed x72, local copies, waits for them, and re-layouts  10.7 us
    slice x1, local copies, waits for them, and re-layouts, shards(): weights = [[w_in[layer, :, j] for j in range(4)] for layer in range(layers)]  8.98 us
    pallas_call x2, Pallas kernels, attend(): pl.pallas_call(functools.partial(attend_kernel, len(pieces), unit, nblk,...  8.38 us
    pallas_call x2, Pallas kernels, turned(): pl.pallas_call(functools.partial(turn_kernel, nblk, block), grid=(1,), ou...  5.2 us
    pallas_call x2, Pallas kernels, shards(): pl.pallas_call(functools.partial(rest_kernel, dh), out_shape=(struct((row...  4.49 us
    pallas_call x2, Pallas kernels, shards(): pl.pallas_call(combine_kernel, out_shape=struct((rows, 2 * width), F32),...  4 us
  transfers between devices with their start and end apart: 31, of which 8 were waited for; matrix products, arithmetic and copies ran while one was open for 4% of the time, Pallas kernels for 10%

profile of v1, /device:TPU:0, one launch (start us, length us, event | category | flops | bytes accessed | tf_op | source)
XLA Modules:
  0.0 138.4 jit_solution(3991439322737858368)
XLA Ops:
  0.0 9.0 %fusion = (bf16[1,512,1,256]{3,2,1,0:T(2,128)(2,1)}, bf16[1,512,1,256]{3,2,1,0:T(2,128)(2,1)}, bf16[1,512,1,256]{3,2,1,0:T(2,128)(2,1)}, bf16[1,512,1,256]{3,2,1...) fusion(bf16[2,512,4,256]{3,2,1,0:T(4,128)(2,1)} %param.12), kind=kLoop, calls=%fused_computation.11 | loop fusion | bytes 4194304 | tf_op jit(solution)/shard_map/slice | solution.py:246
  9.0 0.9 copy_bitcast_fusion.6
  9.9 2.1 %shard_map.94 = (bf16[128,512]{1,0:T(8,128)(2,1)}, bf16[128,256]{1,0:T(8,128)(2,1)}) custom-call(bf16[128,512]{1,0:T(8,128)(2,1)} %stream_ref.1, bf16[512,256]{1,0:T(8,128)(2,1)} %get-tuple-element.74.w_ref), custom_call_target="tpu_custom_call" | custom-call | flops 100000000 | bytes 1000000 | tf_op jit(solution)/shard_map/pallas_call | solution.py:248
  12.0 3.0 %collective-permute-start = (bf16[128,256]{1,0:T(8,128)(2,1)}, bf16[128,256]{1,0:T(8,128)(2,1)S(1)}, u32[]{:S(2)}, u32[]{:S(2)}) collective-permute-start(bf16[128,256]{1,0:T(8,128)(2,1)} %get-tuple-element.34.rest_0_.q_ref), channel_id=1, source_target_pairs={{0,2},{2,0},{4,6},{6,4},{8,10},{10,8},{12,14},{14,12},{1,3},{3,1},... | collective-permute-start | bytes 196616 | tf_op jit(solution)/shard_map/ppermute | solution.py:243
  15.0 1.6 %collective-permute-start.1 = (bf16[128,256]{1,0:T(8,128)(2,1)}, bf16[128,256]{1,0:T(8,128)(2,1)S(1)}, u32[]{:S(2)}, u32[]{:S(2)}) collective-permute-start(bf16[128,256]{1,0:T(8,128)(2,1)} %get-tuple-element.34.rest_0_.q_ref), channel_id=1, source_target_pairs={{0,4},{2,6},{4,0},{6,2},{8,12},{10,14},{12,8},{14,10},{1,5},{3,7},... | collective-permute-start | bytes 196616 | tf_op jit(solution)/shard_map/ppermute | solution.py:243
  16.6 3.0 %collective-permute-start.3 = (bf16[128,256]{1,0:T(8,128)(2,1)}, bf16[128,256]{1,0:T(8,128)(2,1)S(1)}, u32[]{:S(2)}, u32[]{:S(2)}) collective-permute-start(bf16[128,256]{1,0:T(8,128)(2,1)} %get-tuple-element.34.rest_0_.q_ref), channel_id=1, source_target_pairs={{0,8},{2,10},{4,12},{6,14},{8,0},{10,2},{12,4},{14,6},{1,9},{3,11}... | collective-permute-start | bytes 196616 | tf_op jit(solution)/shard_map/ppermute | solution.py:243
  19.6 1.3 collective-permute-start.4
  21.5 0.6 reshape.15.bucket_ref
  22.1 0.1 tile.21.rab_ref
  22.2 2.6 %shard_map.93.vt_ref = bf16[9,256,256]{2,1,0:T(8,128)(2,1)} custom-call(s32[1]{0:T(128)S(6)} %copy.36.len_ref, bf16[2,2048,256]{2,1,0:T(8,128)(2,1)} %v_ref.3), custom_call_target="tpu_custom_call" | custom-call | flops 100000000 | bytes 2000000 | tf_op jit(solution)/shard_map/pallas_call | solution.py:215
  24.8 2.4 %shard_map.91 = (bf16[2048,128]{1,0:T(8,128)(2,1)}, s32[8,10]{1,0:T(8,128)}) custom-call(s32[1]{0:T(128)S(6)} %copy.36.len_ref, s32[8,8]{1,0:T(8,128)} %vis_ref.1, s32[8,256]{1,0:T(8,128)} %reshape.15.bucket_ref), custom_call_target="tpu_custom_call" | custom-call | flops 100000000 | bytes 1000000 | tf_op jit(solution)/shard_map/pallas_call | solution.py:206
  27.3 3.7 %collective-permute-start.5 = (bf16[128,256]{1,0:T(8,128)(2,1)S(1)}, bf16[128,256]{1,0:T(8,128)(2,1)S(1)}, u32[]{:S(2)}, u32[]{:S(2)}) collective-permute-start(bf16[128,256]{1,0:T(8,128)(2,1)S(1)} %copy-done.4), channel_id=1, source_target_pairs={{0,12},{2,14},{4,8},{6,10},{8,4},{10,6},{12,0},{14,2},{1,13},{3,15... | collective-permute-start | bytes 196616 | tf_op jit(solution)/shard_map/ppermute | solution.py:243
  31.0 0.0 collective-permute-start.6
  31.0 2.4 %collective-permute-done.5.rest_6_ = bf16[128,256]{1,0:T(8,128)(2,1)S(1)} collective-permute-done((bf16[128,256]{1,0:T(8,128)(2,1)S(1)}, bf16[128,256]{1,0:T(8,128)(2,1)S(1)}, u32[]{:S(2)}, u32[]{:S(2)}) %collective-permute-start.5) | collective-permute-done | bytes 65568 | tf_op jit(solution)/shard_map/ppermute | solution.py:243
  33.4 4.5 %collective-permute-done.6.rest_7_ = bf16[128,256]{1,0:T(8,128)(2,1)S(1)} collective-permute-done((bf16[128,256]{1,0:T(8,128)(2,1)S(1)}, bf16[128,256]{1,0:T(8,128)(2,1)S(1)}, u32[]{:S(2)}, u32[]{:S(2)}) %collective-permute-start.6) | collective-permute-done | bytes 65568 | tf_op jit(solution)/shard_map/ppermute | solution.py:243
  37.9 1.3 copy-done
  39.2 1.0 copy-done.7
  40.2 0.7 copy-done.9
  40.9 4.2 %shard_map.95 = (bf16[128,256]{1,0:T(8,128)(2,1)S(1)}, bf16[128,256]{1,0:T(8,128)(2,1)S(1)}, bf16[128,256]{1,0:T(8,128)(2,1)S(1)}, bf16[128,256]{1,0:T(8,128)(2,...) custom-call(s32[8]{0:T(128)S(1)} %iota_xor_fusion.order_ref, ...), custom_call_target="tpu_custom_call" | custom-call | flops 10000000000 | bytes 4000000 | tf_op jit(solution)/shard_map/pallas_call | solution.py:227
  45.1 0.6 copy-done.2
  45.8 7.1 %collective-permute-start.10 = (bf16[128,256]{1,0:T(8,128)(2,1)S(1)}, bf16[128,256]{1,0:T(8,128)(2,1)S(1)}, u32[]{:S(2)}, u32[]{:S(2)}) collective-permute-start(bf16[128,256]{1,0:T(8,128)(2,1)S(1)} %get-tuple-element.39), channel_id=1, source_target_pairs={{0,8},{2,10},{4,12},{6,14},{8,0},{10,2},{12,4},{14,6},{1,9},{3,11}... | collective-permute-start | bytes 196616 | tf_op jit(solution)/shard_map/ppermute | solution.py:243
  52.9 5.2 %collective-permute-start.11 = (bf16[128,256]{1,0:T(8,128)(2,1)S(1)}, bf16[128,256]{1,0:T(8,128)(2,1)S(1)}, u32[]{:S(2)}, u32[]{:S(2)}) collective-permute-start(bf16[128,256]{1,0:T(8,128)(2,1)S(1)} %get-tuple-element.40), channel_id=1, source_target_pairs={{0,10},{2,8},{4,14},{6,12},{8,2},{10,0},{12,6},{14,4},{1,11},{3,9}... | collective-permute-start | bytes 196616 | tf_op jit(solution)/shard_map/ppermute | solution.py:243
  58.0 3.8 %collective-permute-start.13 = (bf16[128,256]{1,0:T(8,128)(2,1)S(1)}, bf16[128,256]{1,0:T(8,128)(2,1)S(1)}, u32[]{:S(2)}, u32[]{:S(2)}) collective-permute-start(bf16[128,256]{1,0:T(8,128)(2,1)S(1)} %get-tuple-element.42), channel_id=1, source_target_pairs={{0,14},{2,12},{4,10},{6,8},{8,6},{10,4},{12,2},{14,0},{1,15},{3,13... | collective-permute-start | bytes 196616 | tf_op jit(solution)/shard_map/ppermute | solution.py:243
  61.9 1.5 %collective-permute-start.7 = (bf16[128,256]{1,0:T(8,128)(2,1)S(1)}, bf16[128,256]{1,0:T(8,128)(2,1)S(1)}, u32[]{:S(2)}, u32[]{:S(2)}) collective-permute-start(bf16[128,256]{1,0:T(8,128)(2,1)S(1)} %get-tuple-element.36), channel_id=1, source_target_pairs={{0,2},{2,0},{4,6},{6,4},{8,10},{10,8},{12,14},{14,12},{1,3},{3,1},... | collective-permute-start | bytes 196616 | tf_op jit(solution)/shard_map/ppermute | solution.py:243
  63.3 1.5 %collective-permute-done.12.refs_6_ = bf16[128,256]{1,0:T(8,128)(2,1)S(1)} collective-permute-done((bf16[128,256]{1,0:T(8,128)(2,1)S(1)}, bf16[128,256]{1,0:T(8,128)(2,1)S(1)}, u32[]{:S(2)}, u32[]{:S(2)}) %collective-permute-start.12) | collective-permute-done | bytes 65568 | tf_op jit(solution)/shard_map/ppermute | solution.py:243
  64.9 4.0 %collective-permute-start.9 = (bf16[128,256]{1,0:T(8,128)(2,1)S(1)}, bf16[128,256]{1,0:T(8,128)(2,1)S(1)}, u32[]{:S(2)}, u32[]{:S(2)}) collective-permute-start(bf16[128,256]{1,0:T(8,128)(2,1)S(1)} %get-tuple-element.38), channel_id=1, source_target_pairs={{0,6},{2,4},{4,2},{6,0},{8,14},{10,12},{12,10},{14,8},{1,7},{3,5},... | collective-permute-start | bytes 196616 | tf_op jit(solution)/shard_map/ppermute | solution.py:243
  68.8 0.9 copy_bitcast_fusion.4
  69.7 2.2 %shard_map.96 = (f32[128,256]{1,0:T(8,128)}, f32[128,256]{1,0:T(8,128)}) custom-call(bf16[128,512]{1,0:T(8,128)(2,1)} %get-tuple-element.43.normed_ref, bf16[128,256]{1,0:T(8,128)(2,1)} %get-tuple-element.34.rest_0_.q_ref, bf16[512,256]{1,0:T(8,128)(2,1)} %get-tuple-element.73.wk_ref, bf16[512,256]{1,0:T(8,128)(2,1)} %get-tuple-element.72.wv_ref, ...), custom_call_target="tpu_custom_call" | custom-call | flops 100000000 | bytes 1000000 | tf_op jit(solution)/shard_map/pallas_call | solution.py:262
  72.1 0.5 copy-done.26
  72.6 0.0 copy-done.28
  72.6 0.0 copy-done.30
  72.7 2.0 %shard_map.97.mine_ref = f32[128,512]{1,0:T(8,128)} custom-call(bf16[128,256]{1,0:T(8,128)(2,1)} %copy-done.2, bf16[128,256]{1,0:T(8,128)(2,1)} %copy-done.28, bf16[128,256]{1,0:T(8,128)(2,1)} %copy-done.30, bf16[128,256]{1,0:T(8,128)(2,1)} %copy-done.32, bf16[128,256]{1,0:T(8,128)(2,1)} %copy-done.19, bf16[128,256]{1,0:T(8,128)(2,1)} %copy-done.20, ...), custom_call_target="tpu_custom_call" | custom-call | flops 1000000 | bytes 1000000 | tf_op jit(solution)/shard_map/pallas_call | solution.py:274
  74.7 1.8 %copy.35 = bf16[1,512,1,256]{3,1,2,0:T(8,128)(2,1)} copy(bf16[1,512,1,256]{3,2,1,0:T(2,128)(2,1)} %get-tuple-element.62) | data formatting | bytes 524288
  76.5 0.7 copy-done.17
  77.2 2.6 %shard_map.98 = (f32[128,512]{1,0:T(8,128)}, bf16[128,512]{1,0:T(8,128)(2,1)}, bf16[128,256]{1,0:T(8,128)(2,1)}) custom-call(s32[1]{0:T(128)} %bitcast.head_ref, f32[128,512]{1,0:T(8,128)} %shard_map.97.mine_ref, f32[128,512]{1,0:T(8,128)} %copy-done.17, bf16[2,256,512]{2,1,0:T(8,128)(2,1)} %wa_ref.3, bf16[2,256,512]{2,1,0:T(8,128)(2,1)} %collective-permute-done.15.wb_ref, ...), custom_call_target="tpu_custom_call" | custom-call | flops 100000000 | bytes 1000000 | tf_op jit(solution)/shard_map/pallas_call | solution.py:292
  79.8 0.6 collective-permute-start.16
  80.4 1.9 %collective-permute-start.17 = (bf16[128,256]{1,0:T(8,128)(2,1)}, bf16[128,256]{1,0:T(8,128)(2,1)S(1)}, u32[]{:S(2)}, u32[]{:S(2)}) collective-permute-start(bf16[128,256]{1,0:T(8,128)(2,1)} %get-tuple-element.46.rest_0_.q_ref), channel_id=1, source_target_pairs={{0,4},{2,6},{4,0},{6,2},{8,12},{10,14},{12,8},{14,10},{1,5},{3,7},... | collective-permute-start | bytes 196616 | tf_op jit(solution)/shard_map/ppermute | solution.py:243
  82.4 1.0 collective-permute-start.18
  83.4 2.9 %collective-permute-start.20 = (bf16[128,256]{1,0:T(8,128)(2,1)}, bf16[128,256]{1,0:T(8,128)(2,1)S(1)}, u32[]{:S(2)}, u32[]{:S(2)}) collective-permute-start(bf16[128,256]{1,0:T(8,128)(2,1)} %get-tuple-element.46.rest_0_.q_ref), channel_id=1, source_target_pairs={{0,10},{2,8},{4,14},{6,12},{8,2},{10,0},{12,6},{14,4},{1,11},{3,9}... | collective-permute-start | bytes 196616 | tf_op jit(solution)/shard_map/ppermute | solution.py:243
  86.3 1.4 %collective-permute-start.21 = (bf16[128,256]{1,0:T(8,128)(2,1)}, bf16[128,256]{1,0:T(8,128)(2,1)S(1)}, u32[]{:S(2)}, u32[]{:S(2)}) collective-permute-start(bf16[128,256]{1,0:T(8,128)(2,1)} %get-tuple-element.46.rest_0_.q_ref), channel_id=1, source_target_pairs={{0,12},{2,14},{4,8},{6,10},{8,4},{10,6},{12,0},{14,2},{1,13},{3,15... | collective-permute-start | bytes 196616 | tf_op jit(solution)/shard_map/ppermute | solution.py:243
  87.7 3.3 %collective-permute-start.22 = (bf16[128,256]{1,0:T(8,128)(2,1)}, bf16[128,256]{1,0:T(8,128)(2,1)S(1)}, u32[]{:S(2)}, u32[]{:S(2)}) collective-permute-start(bf16[128,256]{1,0:T(8,128)(2,1)} %get-tuple-element.46.rest_0_.q_ref), channel_id=1, source_target_pairs={{0,14},{2,12},{4,10},{6,8},{8,6},{10,4},{12,2},{14,0},{1,15},{3,13... | collective-permute-start | bytes 196616 | tf_op jit(solution)/shard_map/ppermute | solution.py:243
  91.0 0.1 tile.9.rab_ref
  91.1 2.6 %shard_map.92.vt_ref = bf16[9,256,256]{2,1,0:T(8,128)(2,1)} custom-call(s32[1]{0:T(128)S(6)} %copy.36.len_ref, bf16[2,2048,256]{2,1,0:T(8,128)(2,1)} %v_ref.3), custom_call_target="tpu_custom_call" | custom-call | flops 100000000 | bytes 2000000 | tf_op jit(solution)/shard_map/pallas_call | solution.py:215
  93.7 0.6 collective-permute-done.19.rest_4_
  94.3 2.1 %collective-permute-done.20.rest_5_ = bf16[128,256]{1,0:T(8,128)(2,1)S(1)} collective-permute-done((bf16[128,256]{1,0:T(8,128)(2,1)}, bf16[128,256]{1,0:T(8,128)(2,1)S(1)}, u32[]{:S(2)}, u32[]{:S(2)}) %collective-permute-start.20) | collective-permute-done | bytes 65568 | tf_op jit(solution)/shard_map/ppermute | solution.py:243
  96.5 1.3 copy-done.1
  97.8 4.2 %shard_map.99 = (bf16[128,256]{1,0:T(8,128)(2,1)S(1)}, bf16[128,256]{1,0:T(8,128)(2,1)S(1)}, bf16[128,256]{1,0:T(8,128)(2,1)S(1)}, bf16[128,256]{1,0:T(8,128)(2,...) custom-call(s32[8]{0:T(128)S(1)} %iota_xor_fusion.order_ref, ...), custom_call_target="tpu_custom_call" | custom-call | flops 10000000000 | bytes 4000000 | tf_op jit(solution)/shard_map/pallas_call | solution.py:227
  102.0 0.6 copy-done.3
  102.6 0.8 collective-permute-start.23
  103.3 12.6 %collective-permute-start.24 = (bf16[128,256]{1,0:T(8,128)(2,1)S(1)}, bf16[128,256]{1,0:T(8,128)(2,1)S(1)}, u32[]{:S(2)}, u32[]{:S(2)}) collective-permute-start(bf16[128,256]{1,0:T(8,128)(2,1)S(1)} %get-tuple-element.49), channel_id=1, source_target_pairs={{0,4},{2,6},{4,0},{6,2},{8,12},{10,14},{12,8},{14,10},{1,5},{3,7},... | collective-permute-start | bytes 196616 | tf_op jit(solution)/shard_map/ppermute | solution.py:243
  116.0 4.2 %collective-permute-start.26 = (bf16[128,256]{1,0:T(8,128)(2,1)S(1)}, bf16[128,256]{1,0:T(8,128)(2,1)S(1)}, u32[]{:S(2)}, u32[]{:S(2)}) collective-permute-start(bf16[128,256]{1,0:T(8,128)(2,1)S(1)} %get-tuple-element.51), channel_id=1, source_target_pairs={{0,8},{2,10},{4,12},{6,14},{8,0},{10,2},{12,4},{14,6},{1,9},{3,11}... | collective-permute-start | bytes 196616 | tf_op jit(solution)/shard_map/ppermute | solution.py:243
  120.2 1.5 %collective-permute-start.27 = (bf16[128,256]{1,0:T(8,128)(2,1)S(1)}, bf16[128,256]{1,0:T(8,128)(2,1)S(1)}, u32[]{:S(2)}, u32[]{:S(2)}) collective-permute-start(bf16[128,256]{1,0:T(8,128)(2,1)S(1)} %get-tuple-element.52), channel_id=1, source_target_pairs={{0,10},{2,8},{4,14},{6,12},{8,2},{10,0},{12,6},{14,4},{1,11},{3,9}... | collective-permute-start | bytes 196616 | tf_op jit(solution)/shard_map/ppermute | solution.py:243
  121.6 2.4 %collective-permute-start.28 = (bf16[128,256]{1,0:T(8,128)(2,1)S(1)}, bf16[128,256]{1,0:T(8,128)(2,1)S(1)}, u32[]{:S(2)}, u32[]{:S(2)}) collective-permute-start(bf16[128,256]{1,0:T(8,128)(2,1)S(1)} %get-tuple-element.53), channel_id=1, source_target_pairs={{0,12},{2,14},{4,8},{6,10},{8,4},{10,6},{12,0},{14,2},{1,13},{3,15... | collective-permute-start | bytes 196616 | tf_op jit(solution)/shard_map/ppermute | solution.py:243
  124.0 1.5 %collective-permute-start.29 = (bf16[128,256]{1,0:T(8,128)(2,1)S(1)}, bf16[128,256]{1,0:T(8,128)(2,1)S(1)}, u32[]{:S(2)}, u32[]{:S(2)}) collective-permute-start(bf16[128,256]{1,0:T(8,128)(2,1)S(1)} %get-tuple-element.54), channel_id=1, source_target_pairs={{0,14},{2,12},{4,10},{6,8},{8,6},{10,4},{12,2},{14,0},{1,15},{3,13... | collective-permute-start | bytes 196616 | tf_op jit(solution)/shard_map/ppermute | solution.py:243
  125.5 0.9 copy_bitcast_fusion
  126.4 0.7 copy.34
  127.2 2.2 %shard_map.100 = (f32[128,256]{1,0:T(8,128)}, f32[128,256]{1,0:T(8,128)}) custom-call(bf16[128,512]{1,0:T(8,128)(2,1)} %get-tuple-element.55.normed_ref, bf16[128,256]{1,0:T(8,128)(2,1)} %get-tuple-element.46.rest_0_.q_ref, bf16[512,256]{1,0:T(8,128)(2,1)} %bitcast.28, bf16[512,256]{1,0:T(8,128)(2,1)} %get-tuple-element.70.wv_ref, ...), custom_call_target="tpu_custom_call" | custom-call | flops 100000000 | bytes 1000000 | tf_op jit(solution)/shard_map/pallas_call | solution.py:262
  129.4 0.8 collective-permute-done.27.refs_5_
  130.3 0.8 collective-permute-done.29.refs_7_
  131.1 0.6 copy-done.31
  131.7 2.0 %shard_map.101.mine_ref = f32[128,512]{1,0:T(8,128)} custom-call(bf16[128,256]{1,0:T(8,128)(2,1)} %copy-done.3, bf16[128,256]{1,0:T(8,128)(2,1)} %copy-done.21, bf16[128,256]{1,0:T(8,128)(2,1)} %copy-done.23, bf16[128,256]{1,0:T(8,128)(2,1)} %copy-done.24, bf16[128,256]{1,0:T(8,128)(2,1)} %copy-done.25, bf16[128,256]{1,0:T(8,128)(2,1)} %copy-done.27, ...), custom_call_target="tpu_custom_call" | custom-call | flops 1000000 | bytes 1000000 | tf_op jit(solution)/shard_map/pallas_call | solution.py:274
  133.7 1.7 %collective-permute-done.30.other_ref = f32[128,512]{1,0:T(8,128)S(1)} collective-permute-done((f32[128,512]{1,0:T(8,128)}, f32[128,512]{1,0:T(8,128)S(1)}, u32[]{:S(2)}, u32[]{:S(2)}) %collective-permute-start.30) | collective-permute-done | bytes 262176 | tf_op jit(solution)/shard_map/ppermute | solution.py:245
  135.4 0.7 copy-done.18
  136.1 2.2 %shard_map.102 = bf16[128,512]{1,0:T(8,128)(2,1)} custom-call(s32[1]{0:T(128)} %bitcast.head_ref, f32[128,512]{1,0:T(8,128)} %shard_map.101.mine_ref, f32[128,512]{1,0:T(8,128)} %copy-done.18, bf16[2,256,512]{2,1,0:T(8,128)(2,1)} %wa_ref.3, bf16[2,256,512]{2,1,0:T(8,128)(2,1)} %collective-permute-done.15.wb_ref, f32[128,512]{1,0:T(8,128)} %get-tuple-element.58.stream_ref), custom_call_target="tpu_custom_call" | custom-call | flops 100000000 | bytes 1000000 | tf_op jit(solution)/shard_map/pallas_call | solution.py:283
  (93 shorter events, 0.2 us)
Async XLA Ops:
  0.0 20.9 %copy-start.34 = (f32[2,32,4]{1,2,0:T(4,128)S(1)}, f32[2,32,4]{1,2,0:T(4,128)}, u32[]{:S(2)}) copy-start(f32[2,32,4]{1,2,0:T(4,128)} %param.14) | copy-start | bytes 3076
  0.0 21.5 %copy-start.33 = (s32[2048]{0:T(1024)S(1)}, s32[2048]{0:T(1024)}, u32[]{:S(2)}) copy-start(s32[2048]{0:T(1024)} %param.16) | copy-start | bytes 24580
  9.9 28.1 %copy-start.6 = (bf16[2,2048,256]{2,1,0:T(8,128)(2,1)S(1)}, bf16[2,2048,256]{2,1,0:T(8,128)(2,1)}, u32[]{:S(2)}) copy-start(bf16[2,2048,256]{2,1,0:T(8,128)(2,1)} %k_ref.3) | copy-start | bytes 6291460
  12.0 15.3 %copy-start.4 = (bf16[128,256]{1,0:T(8,128)(2,1)S(1)}, bf16[128,256]{1,0:T(8,128)(2,1)}, u32[]{:S(2)}) copy-start(bf16[128,256]{1,0:T(8,128)(2,1)} %get-tuple-element.34.rest_0_.q_ref) | copy-start | bytes 196612
  12.0 15.2 %collective-permute-start = (bf16[128,256]{1,0:T(8,128)(2,1)}, bf16[128,256]{1,0:T(8,128)(2,1)S(1)}, u32[]{:S(2)}, u32[]{:S(2)}) collective-permute-start(bf16[128,256]{1,0:T(8,128)(2,1)} %get-tuple-element.34.rest_0_.q_ref), channel_id=1, source_target_pairs={{0,2},{2,0},{4,6},{6,4},{8,10},{10,8},{12,14},{14,12},{1,3},{3,1},... | collective-permute-start | bytes 196616 | tf_op jit(solution)/shard_map/ppermute | solution.py:243
  15.0 15.9 %collective-permute-start.1 = (bf16[128,256]{1,0:T(8,128)(2,1)}, bf16[128,256]{1,0:T(8,128)(2,1)S(1)}, u32[]{:S(2)}, u32[]{:S(2)}) collective-permute-start(bf16[128,256]{1,0:T(8,128)(2,1)} %get-tuple-element.34.rest_0_.q_ref), channel_id=1, source_target_pairs={{0,4},{2,6},{4,0},{6,2},{8,12},{10,14},{12,8},{14,10},{1,5},{3,7},... | collective-permute-start | bytes 196616 | tf_op jit(solution)/shard_map/ppermute | solution.py:243
  16.6 14.4 %collective-permute-start.2 = (bf16[128,256]{1,0:T(8,128)(2,1)}, bf16[128,256]{1,0:T(8,128)(2,1)S(1)}, u32[]{:S(2)}, u32[]{:S(2)}) collective-permute-start(bf16[128,256]{1,0:T(8,128)(2,1)} %get-tuple-element.34.rest_0_.q_ref), channel_id=1, source_target_pairs={{0,6},{2,4},{4,2},{6,0},{8,14},{10,12},{12,10},{14,8},{1,7},{3,5},... | collective-permute-start | bytes 196616 | tf_op jit(solution)/shard_map/ppermute | solution.py:243
  16.6 14.4 %collective-permute-start.3 = (bf16[128,256]{1,0:T(8,128)(2,1)}, bf16[128,256]{1,0:T(8,128)(2,1)S(1)}, u32[]{:S(2)}, u32[]{:S(2)}) collective-permute-start(bf16[128,256]{1,0:T(8,128)(2,1)} %get-tuple-element.34.rest_0_.q_ref), channel_id=1, source_target_pairs={{0,8},{2,10},{4,12},{6,14},{8,0},{10,2},{12,4},{14,6},{1,9},{3,11}... | collective-permute-start | bytes 196616 | tf_op jit(solution)/shard_map/ppermute | solution.py:243
  19.6 11.4 %collective-permute-start.4 = (bf16[128,256]{1,0:T(8,128)(2,1)}, bf16[128,256]{1,0:T(8,128)(2,1)S(1)}, u32[]{:S(2)}, u32[]{:S(2)}) collective-permute-start(bf16[128,256]{1,0:T(8,128)(2,1)} %get-tuple-element.34.rest_0_.q_ref), channel_id=1, source_target_pairs={{0,10},{2,8},{4,14},{6,12},{8,2},{10,0},{12,6},{14,4},{1,11},{3,9}... | collective-permute-start | bytes 196616 | tf_op jit(solution)/shard_map/ppermute | solution.py:243
  27.3 6.1 %collective-permute-start.5 = (bf16[128,256]{1,0:T(8,128)(2,1)S(1)}, bf16[128,256]{1,0:T(8,128)(2,1)S(1)}, u32[]{:S(2)}, u32[]{:S(2)}) collective-permute-start(bf16[128,256]{1,0:T(8,128)(2,1)S(1)} %copy-done.4), channel_id=1, source_target_pairs={{0,12},{2,14},{4,8},{6,10},{8,4},{10,6},{12,0},{14,2},{1,13},{3,15... | collective-permute-start | bytes 196616 | tf_op jit(solution)/shard_map/ppermute | solution.py:243
  31.0 7.0 %collective-permute-start.6 = (bf16[128,256]{1,0:T(8,128)(2,1)S(1)}, bf16[128,256]{1,0:T(8,128)(2,1)S(1)}, u32[]{:S(2)}, u32[]{:S(2)}) collective-permute-start(bf16[128,256]{1,0:T(8,128)(2,1)S(1)} %copy-done.4), channel_id=1, source_target_pairs={{0,14},{2,12},{4,10},{6,8},{8,6},{10,4},{12,2},{14,0},{1,15},{3,13... | collective-permute-start | bytes 196616 | tf_op jit(solution)/shard_map/ppermute | solution.py:243
  37.9 1.3 copy-start
  39.2 1.0 copy-start.7
  40.2 0.7 copy-start.9
  40.9 17.1 %copy-start.11 = (bf16[2,256,512]{2,1,0:T(8,128)(2,1)S(1)}, bf16[2,256,512]{2,1,0:T(8,128)(2,1)}, u32[]{:S(2)}) copy-start(bf16[2,256,512]{2,1,0:T(8,128)(2,1)} %wa_ref.3) | copy-start | bytes 1572868
  40.9 27.9 %copy-start.14 = (bf16[1,512,1,256]{3,2,1,0:T(2,128)(2,1)S(1)}, bf16[1,512,1,256]{3,2,1,0:T(2,128)(2,1)}, u32[]{:S(2)}) copy-start(bf16[1,512,1,256]{3,2,1,0:T(2,128)(2,1)} %get-tuple-element.63) | copy-start | bytes 786436
  40.9 27.9 %copy-start.15 = (bf16[1,512,1,256]{3,2,1,0:T(2,128)(2,1)S(1)}, bf16[1,512,1,256]{3,2,1,0:T(2,128)(2,1)}, u32[]{:S(2)}) copy-start(bf16[1,512,1,256]{3,2,1,0:T(2,128)(2,1)} %get-tuple-element.64) | copy-start | bytes 786436
  45.1 0.6 copy-start.2
  45.8 16.1 %collective-permute-start.10 = (bf16[128,256]{1,0:T(8,128)(2,1)S(1)}, bf16[128,256]{1,0:T(8,128)(2,1)S(1)}, u32[]{:S(2)}, u32[]{:S(2)}) collective-permute-start(bf16[128,256]{1,0:T(8,128)(2,1)S(1)} %get-tuple-element.39), channel_id=1, source_target_pairs={{0,8},{2,10},{4,12},{6,14},{8,0},{10,2},{12,4},{14,6},{1,9},{3,11}... | collective-permute-start | bytes 196616 | tf_op jit(solution)/shard_map/ppermute | solution.py:243
  52.9 10.5 %collective-permute-start.11 = (bf16[128,256]{1,0:T(8,128)(2,1)S(1)}, bf16[128,256]{1,0:T(8,128)(2,1)S(1)}, u32[]{:S(2)}, u32[]{:S(2)}) collective-permute-start(bf16[128,256]{1,0:T(8,128)(2,1)S(1)} %get-tuple-element.40), channel_id=1, source_target_pairs={{0,10},{2,8},{4,14},{6,12},{8,2},{10,0},{12,6},{14,4},{1,11},{3,9}... | collective-permute-start | bytes 196616 | tf_op jit(solution)/shard_map/ppermute | solution.py:243
  58.0 6.8 %collective-permute-start.12 = (bf16[128,256]{1,0:T(8,128)(2,1)S(1)}, bf16[128,256]{1,0:T(8,128)(2,1)S(1)}, u32[]{:S(2)}, u32[]{:S(2)}) collective-permute-start(bf16[128,256]{1,0:T(8,128)(2,1)S(1)} %get-tuple-element.41), channel_id=1, source_target_pairs={{0,12},{2,14},{4,8},{6,10},{8,4},{10,6},{12,0},{14,2},{1,13},{3,15... | collective-permute-start | bytes 196616 | tf_op jit(solution)/shard_map/ppermute | solution.py:243
  58.0 18.4 %collective-permute-start.15 = (bf16[2,256,512]{2,1,0:T(8,128)(2,1)S(1)}, bf16[2,256,512]{2,1,0:T(8,128)(2,1)}, u32[]{:S(2)}, u32[]{:S(2)}) collective-permute-start(bf16[2,256,512]{2,1,0:T(8,128)(2,1)S(1)} %copy-done.11), channel_id=1, source_target_pairs={{0,1},{1,0},{2,3},{3,2},{4,5},{5,4},{6,7},{7,6},{8,9},{9,8},{10,11... | collective-permute-start | bytes 1572872 | tf_op jit(solution)/shard_map/ppermute | solution.py:245
  58.0 13.9 %collective-permute-start.13 = (bf16[128,256]{1,0:T(8,128)(2,1)S(1)}, bf16[128,256]{1,0:T(8,128)(2,1)S(1)}, u32[]{:S(2)}, u32[]{:S(2)}) collective-permute-start(bf16[128,256]{1,0:T(8,128)(2,1)S(1)} %get-tuple-element.42), channel_id=1, source_target_pairs={{0,14},{2,12},{4,10},{6,8},{8,6},{10,4},{12,2},{14,0},{1,15},{3,13... | collective-permute-start | bytes 196616 | tf_op jit(solution)/shard_map/ppermute | solution.py:243
  61.9 10.2 %copy-start.19 = (bf16[128,256]{1,0:T(8,128)(2,1)}, bf16[128,256]{1,0:T(8,128)(2,1)S(1)}, u32[]{:S(2)}) copy-start(bf16[128,256]{1,0:T(8,128)(2,1)S(1)} %collective-permute-done.10.refs_4_) | copy-start | bytes 196612
  61.9 10.1 %collective-permute-start.7 = (bf16[128,256]{1,0:T(8,128)(2,1)S(1)}, bf16[128,256]{1,0:T(8,128)(2,1)S(1)}, u32[]{:S(2)}, u32[]{:S(2)}) collective-permute-start(bf16[128,256]{1,0:T(8,128)(2,1)S(1)} %get-tuple-element.36), channel_id=1, source_target_pairs={{0,2},{2,0},{4,6},{6,4},{8,10},{10,8},{12,14},{14,12},{1,3},{3,1},... | collective-permute-start | bytes 196616 | tf_op jit(solution)/shard_map/ppermute | solution.py:243
  63.3 8.7 %copy-start.20 = (bf16[128,256]{1,0:T(8,128)(2,1)}, bf16[128,256]{1,0:T(8,128)(2,1)S(1)}, u32[]{:S(2)}) copy-start(bf16[128,256]{1,0:T(8,128)(2,1)S(1)} %collective-permute-done.11.refs_5_) | copy-start | bytes 196612
  63.3 8.7 %collective-permute-start.8 = (bf16[128,256]{1,0:T(8,128)(2,1)S(1)}, bf16[128,256]{1,0:T(8,128)(2,1)S(1)}, u32[]{:S(2)}, u32[]{:S(2)}) collective-permute-start(bf16[128,256]{1,0:T(8,128)(2,1)S(1)} %get-tuple-element.37), channel_id=1, source_target_pairs={{0,4},{2,6},{4,0},{6,2},{8,12},{10,14},{12,8},{14,10},{1,5},{3,7},... | collective-permute-start | bytes 196616 | tf_op jit(solution)/shard_map/ppermute | solution.py:243
  64.9 7.2 %copy-start.22 = (bf16[128,256]{1,0:T(8,128)(2,1)}, bf16[128,256]{1,0:T(8,128)(2,1)S(1)}, u32[]{:S(2)}) copy-start(bf16[128,256]{1,0:T(8,128)(2,1)S(1)} %collective-permute-done.12.refs_6_) | copy-start | bytes 196612
  64.9 7.2 %collective-permute-start.9 = (bf16[128,256]{1,0:T(8,128)(2,1)S(1)}, bf16[128,256]{1,0:T(8,128)(2,1)S(1)}, u32[]{:S(2)}, u32[]{:S(2)}) collective-permute-start(bf16[128,256]{1,0:T(8,128)(2,1)S(1)} %get-tuple-element.38), channel_id=1, source_target_pairs={{0,6},{2,4},{4,2},{6,0},{8,14},{10,12},{12,10},{14,8},{1,7},{3,5},... | collective-permute-start | bytes 196616 | tf_op jit(solution)/shard_map/ppermute | solution.py:243
  72.0 0.6 copy-start.28
  72.0 0.6 copy-start.30
  72.0 0.6 copy-start.32
  74.7 1.8 %collective-permute-start.14 = (f32[128,512]{1,0:T(8,128)}, f32[128,512]{1,0:T(8,128)S(1)}, u32[]{:S(2)}, u32[]{:S(2)}) collective-permute-start(f32[128,512]{1,0:T(8,128)} %shard_map.97.mine_ref), channel_id=1, source_target_pairs={{0,1},{1,0},{2,3},{3,2},{4,5},{5,4},{6,7},{7,6},{8,9},{9,8},{10,11... | collective-permute-start | bytes 786440 | tf_op jit(solution)/shard_map/ppermute | solution.py:245
  76.5 0.7 copy-start.17
  79.8 16.7 %copy-start.5 = (bf16[128,256]{1,0:T(8,128)(2,1)S(1)}, bf16[128,256]{1,0:T(8,128)(2,1)}, u32[]{:S(2)}) copy-start(bf16[128,256]{1,0:T(8,128)(2,1)} %get-tuple-element.46.rest_0_.q_ref) | copy-start | bytes 196612
  79.8 16.7 %copy-start.8 = (bf16[2048,128]{1,0:T(8,128)(2,1)S(1)}, bf16[2048,128]{1,0:T(8,128)(2,1)}, u32[]{:S(2)}) copy-start(bf16[2048,128]{1,0:T(8,128)(2,1)} %get-tuple-element.33.oh_ref) | copy-start | bytes 1572868
  79.8 16.7 %copy-start.10 = (s32[8,10]{1,0:T(8,128)S(1)}, s32[8,10]{1,0:T(8,128)}, u32[]{:S(2)}) copy-start(s32[8,10]{1,0:T(8,128)} %get-tuple-element.32.list_ref) | copy-start | bytes 964
  79.8 6.5 %collective-permute-start.16 = (bf16[128,256]{1,0:T(8,128)(2,1)}, bf16[128,256]{1,0:T(8,128)(2,1)S(1)}, u32[]{:S(2)}, u32[]{:S(2)}) collective-permute-start(bf16[128,256]{1,0:T(8,128)(2,1)} %get-tuple-element.46.rest_0_.q_ref), channel_id=1, source_target_pairs={{0,2},{2,0},{4,6},{6,4},{8,10},{10,8},{12,14},{14,12},{1,3},{3,1},... | collective-permute-start | bytes 196616 | tf_op jit(solution)/shard_map/ppermute | solution.py:243
  80.4 7.2 %collective-permute-start.17 = (bf16[128,256]{1,0:T(8,128)(2,1)}, bf16[128,256]{1,0:T(8,128)(2,1)S(1)}, u32[]{:S(2)}, u32[]{:S(2)}) collective-permute-start(bf16[128,256]{1,0:T(8,128)(2,1)} %get-tuple-element.46.rest_0_.q_ref), channel_id=1, source_target_pairs={{0,4},{2,6},{4,0},{6,2},{8,12},{10,14},{12,8},{14,10},{1,5},{3,7},... | collective-permute-start | bytes 196616 | tf_op jit(solution)/shard_map/ppermute | solution.py:243
  82.4 11.3 %collective-permute-start.18 = (bf16[128,256]{1,0:T(8,128)(2,1)}, bf16[128,256]{1,0:T(8,128)(2,1)S(1)}, u32[]{:S(2)}, u32[]{:S(2)}) collective-permute-start(bf16[128,256]{1,0:T(8,128)(2,1)} %get-tuple-element.46.rest_0_.q_ref), channel_id=1, source_target_pairs={{0,6},{2,4},{4,2},{6,0},{8,14},{10,12},{12,10},{14,8},{1,7},{3,5},... | collective-permute-start | bytes 196616 | tf_op jit(solution)/shard_map/ppermute | solution.py:243
  83.4 11.0 %collective-permute-start.19 = (bf16[128,256]{1,0:T(8,128)(2,1)}, bf16[128,256]{1,0:T(8,128)(2,1)S(1)}, u32[]{:S(2)}, u32[]{:S(2)}) collective-permute-start(bf16[128,256]{1,0:T(8,128)(2,1)} %get-tuple-element.46.rest_0_.q_ref), channel_id=1, source_target_pairs={{0,8},{2,10},{4,12},{6,14},{8,0},{10,2},{12,4},{14,6},{1,9},{3,11}... | collective-permute-start | bytes 196616 | tf_op jit(solution)/shard_map/ppermute | solution.py:243
  83.4 13.1 %collective-permute-start.20 = (bf16[128,256]{1,0:T(8,128)(2,1)}, bf16[128,256]{1,0:T(8,128)(2,1)S(1)}, u32[]{:S(2)}, u32[]{:S(2)}) collective-permute-start(bf16[128,256]{1,0:T(8,128)(2,1)} %get-tuple-element.46.rest_0_.q_ref), channel_id=1, source_target_pairs={{0,10},{2,8},{4,14},{6,12},{8,2},{10,0},{12,6},{14,4},{1,11},{3,9}... | collective-permute-start | bytes 196616 | tf_op jit(solution)/shard_map/ppermute | solution.py:243
  86.3 10.2 %collective-permute-start.21 = (bf16[128,256]{1,0:T(8,128)(2,1)}, bf16[128,256]{1,0:T(8,128)(2,1)S(1)}, u32[]{:S(2)}, u32[]{:S(2)}) collective-permute-start(bf16[128,256]{1,0:T(8,128)(2,1)} %get-tuple-element.46.rest_0_.q_ref), channel_id=1, source_target_pairs={{0,12},{2,14},{4,8},{6,10},{8,4},{10,6},{12,0},{14,2},{1,13},{3,15... | collective-permute-start | bytes 196616 | tf_op jit(solution)/shard_map/ppermute | solution.py:243
  87.7 8.8 %collective-permute-start.22 = (bf16[128,256]{1,0:T(8,128)(2,1)}, bf16[128,256]{1,0:T(8,128)(2,1)S(1)}, u32[]{:S(2)}, u32[]{:S(2)}) collective-permute-start(bf16[128,256]{1,0:T(8,128)(2,1)} %get-tuple-element.46.rest_0_.q_ref), channel_id=1, source_target_pairs={{0,14},{2,12},{4,10},{6,8},{8,6},{10,4},{12,2},{14,0},{1,15},{3,13... | collective-permute-start | bytes 196616 | tf_op jit(solution)/shard_map/ppermute | solution.py:243
  96.5 1.3 copy-start.1
  97.8 27.8 %copy-start.12 = (bf16[1,512,1,256]{3,2,1,0:T(2,128)(2,1)S(1)}, bf16[1,512,1,256]{3,2,1,0:T(2,128)(2,1)}, u32[]{:S(2)}) copy-start(bf16[1,512,1,256]{3,2,1,0:T(2,128)(2,1)} %get-tuple-element.59) | copy-start | bytes 786436
  97.8 27.8 %copy-start.13 = (bf16[1,512,1,256]{3,2,1,0:T(2,128)(2,1)S(1)}, bf16[1,512,1,256]{3,2,1,0:T(2,128)(2,1)}, u32[]{:S(2)}) copy-start(bf16[1,512,1,256]{3,2,1,0:T(2,128)(2,1)} %get-tuple-element.60) | copy-start | bytes 786436
  97.8 28.6 %copy-start.16 = (bf16[1,512,1,256]{3,2,1,0:T(2,128)(2,1)S(1)}, bf16[1,512,1,256]{3,2,1,0:T(2,128)(2,1)}, u32[]{:S(2)}) copy-start(bf16[1,512,1,256]{3,2,1,0:T(2,128)(2,1)} %get-tuple-element.61) | copy-start | bytes 786436
  102.6 19.1 %collective-permute-start.23 = (bf16[128,256]{1,0:T(8,128)(2,1)S(1)}, bf16[128,256]{1,0:T(8,128)(2,1)S(1)}, u32[]{:S(2)}, u32[]{:S(2)}) collective-permute-start(bf16[128,256]{1,0:T(8,128)(2,1)S(1)} %get-tuple-element.48), channel_id=1, source_target_pairs={{0,2},{2,0},{4,6},{6,4},{8,10},{10,8},{12,14},{14,12},{1,3},{3,1},... | collective-permute-start | bytes 196616 | tf_op jit(solution)/shard_map/ppermute | solution.py:243
  103.3 20.7 %collective-permute-start.24 = (bf16[128,256]{1,0:T(8,128)(2,1)S(1)}, bf16[128,256]{1,0:T(8,128)(2,1)S(1)}, u32[]{:S(2)}, u32[]{:S(2)}) collective-permute-start(bf16[128,256]{1,0:T(8,128)(2,1)S(1)} %get-tuple-element.49), channel_id=1, source_target_pairs={{0,4},{2,6},{4,0},{6,2},{8,12},{10,14},{12,8},{14,10},{1,5},{3,7},... | collective-permute-start | bytes 196616 | tf_op jit(solution)/shard_map/ppermute | solution.py:243
  116.0 13.4 %collective-permute-start.25 = (bf16[128,256]{1,0:T(8,128)(2,1)S(1)}, bf16[128,256]{1,0:T(8,128)(2,1)S(1)}, u32[]{:S(2)}, u32[]{:S(2)}) collective-permute-start(bf16[128,256]{1,0:T(8,128)(2,1)S(1)} %get-tuple-element.50), channel_id=1, source_target_pairs={{0,6},{2,4},{4,2},{6,0},{8,14},{10,12},{12,10},{14,8},{1,7},{3,5},... | collective-permute-start | bytes 196616 | tf_op jit(solution)/shard_map/ppermute | solution.py:243
  116.0 13.5 %collective-permute-start.26 = (bf16[128,256]{1,0:T(8,128)(2,1)S(1)}, bf16[128,256]{1,0:T(8,128)(2,1)S(1)}, u32[]{:S(2)}, u32[]{:S(2)}) collective-permute-start(bf16[128,256]{1,0:T(8,128)(2,1)S(1)} %get-tuple-element.51), channel_id=1, source_target_pairs={{0,8},{2,10},{4,12},{6,14},{8,0},{10,2},{12,4},{14,6},{1,9},{3,11}... | collective-permute-start | bytes 196616 | tf_op jit(solution)/shard_map/ppermute | solution.py:243
  120.2 10.1 %collective-permute-start.27 = (bf16[128,256]{1,0:T(8,128)(2,1)S(1)}, bf16[128,256]{1,0:T(8,128)(2,1)S(1)}, u32[]{:S(2)}, u32[]{:S(2)}) collective-permute-start(bf16[128,256]{1,0:T(8,128)(2,1)S(1)} %get-tuple-element.52), channel_id=1, source_target_pairs={{0,10},{2,8},{4,14},{6,12},{8,2},{10,0},{12,6},{14,4},{1,11},{3,9}... | collective-permute-start | bytes 196616 | tf_op jit(solution)/shard_map/ppermute | solution.py:243
  121.6 9.4 %copy-start.21 = (bf16[128,256]{1,0:T(8,128)(2,1)}, bf16[128,256]{1,0:T(8,128)(2,1)S(1)}, u32[]{:S(2)}) copy-start(bf16[128,256]{1,0:T(8,128)(2,1)S(1)} %collective-permute-done.23.refs_1_) | copy-start | bytes 196612
  121.6 8.6 %collective-permute-start.28 = (bf16[128,256]{1,0:T(8,128)(2,1)S(1)}, bf16[128,256]{1,0:T(8,128)(2,1)S(1)}, u32[]{:S(2)}, u32[]{:S(2)}) collective-permute-start(bf16[128,256]{1,0:T(8,128)(2,1)S(1)} %get-tuple-element.53), channel_id=1, source_target_pairs={{0,12},{2,14},{4,8},{6,10},{8,4},{10,6},{12,0},{14,2},{1,13},{3,15... | collective-permute-start | bytes 196616 | tf_op jit(solution)/shard_map/ppermute | solution.py:243
  124.0 7.1 %copy-start.23 = (bf16[128,256]{1,0:T(8,128)(2,1)}, bf16[128,256]{1,0:T(8,128)(2,1)S(1)}, u32[]{:S(2)}) copy-start(bf16[128,256]{1,0:T(8,128)(2,1)S(1)} %collective-permute-done.24.refs_2_) | copy-start | bytes 196612
  124.0 7.1 %collective-permute-start.29 = (bf16[128,256]{1,0:T(8,128)(2,1)S(1)}, bf16[128,256]{1,0:T(8,128)(2,1)S(1)}, u32[]{:S(2)}, u32[]{:S(2)}) collective-permute-start(bf16[128,256]{1,0:T(8,128)(2,1)S(1)} %get-tuple-element.54), channel_id=1, source_target_pairs={{0,14},{2,12},{4,10},{6,8},{8,6},{10,4},{12,2},{14,0},{1,15},{3,13... | collective-permute-start | bytes 196616 | tf_op jit(solution)/shard_map/ppermute | solution.py:243
  129.4 1.7 %copy-start.24 = (bf16[128,256]{1,0:T(8,128)(2,1)}, bf16[128,256]{1,0:T(8,128)(2,1)S(1)}, u32[]{:S(2)}) copy-start(bf16[128,256]{1,0:T(8,128)(2,1)S(1)} %collective-permute-done.25.refs_3_) | copy-start | bytes 196612
  129.4 1.7 %copy-start.25 = (bf16[128,256]{1,0:T(8,128)(2,1)}, bf16[128,256]{1,0:T(8,128)(2,1)S(1)}, u32[]{:S(2)}) copy-start(bf16[128,256]{1,0:T(8,128)(2,1)S(1)} %collective-permute-done.26.refs_4_) | copy-start | bytes 196612
  130.3 0.8 copy-start.27
  130.3 0.8 copy-start.29
  131.1 0.6 copy-start.31
  133.7 1.7 %collective-permute-start.30 = (f32[128,512]{1,0:T(8,128)}, f32[128,512]{1,0:T(8,128)S(1)}, u32[]{:S(2)}, u32[]{:S(2)}) collective-permute-start(f32[128,512]{1,0:T(8,128)} %shard_map.101.mine_ref), channel_id=1, source_target_pairs={{0,1},{1,0},{2,3},{3,2},{4,5},{5,4},{6,7},{7,6},{8,9},{9,8},{10,11... | collective-permute-start | bytes 786440 | tf_op jit(solution)/shard_map/ppermute | solution.py:245
  135.4 0.7 copy-start.18
  (2 other events, 1.2 us)
